TPU v7x, 512 devices: a whole 4x8x8 slice. The times are simulated.
512 devices in a mesh: row: 32 (over x, y), col: 16 (over z, core).
Axes of the slice: x: 4, y: 8, z: 8, core: 2. Of those that a mesh axis runs over, the one named last changes fastest.
Arguments:
- matrix: float32 [8192, 8192], P('row', 'col'), may hold values from -6 to 6
- panel: float32 [8192, 128], P('col'), may hold values from -6 to 6
Outputs:
- updated: float32 [8192, 8192], P('row', 'col')
- band: float32 [128, 128], replicated
All inputs are finite; a program needn't handle non-finite values.
Results may differ from a plain program's by a relative error of at most 0.0002.
Values sent between devices are 32-bit elements; how exact they have to be, the bound alone decides.
A program may use at most 64 MiB of HBM per device.

v0:
```python
import jax
import jax.numpy as jnp
from jax import lax
from jax.sharding import PartitionSpec as P

NS_STEPS = 6


def broadcast(block, axis, owner):
    block = jnp.where(lax.axis_index(axis) == owner, block, jnp.zeros_like(block))
    return lax.psum(block, axis)


def multiply(left_mat, right_mat):
    return jnp.dot(left_mat, right_mat, precision=lax.Precision.HIGHEST)


def factor_lower(gram):
    width = gram.shape[0]
    counter = jnp.arange(width, dtype=jnp.int32)

    def column_step(index, lower):
        unit = (counter == index).astype(jnp.float32)
        row_vals = multiply(unit[None, :], lower)[0]
        source = multiply(gram, unit[:, None])[:, 0]
        vector = source - multiply(lower, row_vals[:, None])[:, 0]
        pivot = jnp.sqrt(jnp.sum(vector * unit))
        below = (counter > index).astype(jnp.float32)
        column = below * vector / pivot + unit * pivot
        return lower + column[:, None] * unit[None, :]

    return lax.fori_loop(0, width, column_step, jnp.zeros_like(gram))


def invert_upper(upper):
    width = upper.shape[0]
    counter = jnp.arange(width, dtype=jnp.int32)

    def row_step(step, inverse):
        index = width - 1 - step
        unit = (counter == index).astype(jnp.float32)
        row_vals = multiply(unit[None, :], upper)[0]
        pivot = jnp.sum(row_vals * unit)
        beyond = row_vals * (counter > index).astype(jnp.float32)
        solved = (unit - multiply(beyond[None, :], inverse)[0]) / pivot
        return inverse + unit[:, None] * solved[None, :]

    return lax.fori_loop(0, width, row_step, jnp.zeros_like(upper))


def per_device(matrix, panel):
    nrow = lax.axis_size("row")
    ncol = lax.axis_size("col")
    rindex = lax.axis_index("row")
    cindex = lax.axis_index("col")
    width = panel.shape[1]
    col_rows = panel.shape[0]
    row_rows = matrix.shape[0]
    top = panel[:width]
    first_col = (cindex == 0).astype(jnp.float32)
    partial_gram = multiply(panel.T, panel)
    gram, first = lax.psum((partial_gram, top * first_col), "col")
    upper = factor_lower(gram).T
    identity = jnp.eye(width, dtype=jnp.float32)
    inv_upper = invert_upper(upper)
    shifted = upper + first
    approx = inv_upper
    for step in range(NS_STEPS):
        approx = multiply(approx, 2.0 * identity - multiply(shifted, approx))
    coupling = multiply(approx, inv_upper.T)
    coupling_t = coupling.T
    refl_col = panel + first_col * jnp.pad(upper, ((0, col_rows - width), (0, 0)))
    ratio = nrow // ncol
    root = rindex // ratio
    offset = rindex % ratio * row_rows
    received = broadcast(refl_col, "col", root)
    refl_row = lax.dynamic_slice_in_dim(received, offset, row_rows, 0)
    right = lax.psum(multiply(matrix, refl_col), "col")
    left_part = multiply(refl_row.T, matrix)
    curv = lax.psum(multiply(left_part, refl_col), ("row", "col"))
    left = lax.psum(left_part, "row")
    applied = multiply(coupling_t, left)
    second = multiply(right - multiply(refl_row, multiply(coupling_t, curv)), coupling)
    updated = matrix - multiply(refl_row, applied) - multiply(second, refl_col.T)
    return (updated, -upper)


def solution(mesh):
    placed = (P("row", "col"), P("col", None))
    return jax.shard_map(
        per_device, mesh=mesh, in_specs=placed, out_specs=(P("row", "col"), P()), check_vma=False
    )
```

profile of v0, /device:TPU:1, one launch (start us, length us, event | category | flops | bytes accessed | tf_op | source)
XLA Modules:
  0.0 1123.9 jit_solution(11541026879659751510)
XLA Ops:
  7.2 2.3 fusion.48
  10.2 111.2 %all-reduce.7.cloned.1.call-done = f32[128,128]{1,0:T(8,128)} async-done(((f32[128,128]{1,0:T(8,128)}), f32[128,128]{1,0:T(8,128)}) %all-reduce.7.cloned.1.call-update) | async-done | bytes 65552 | tf_op jit(solution)/shard_map/psum | solution.py:62
  121.4 363.3 %while.30 = (s32[]{:T(128)}, f32[128,128]{1,0:T(8,128)S(1)}, f32[128,128]{1,0:T(8,128)}, s32[]{:T(128)}, s32[]{:T(128)}) while((s32[]{:T(128)}, f32[128,128]{1,0:T(8,128)S(1)}, f32[128,128]{1,0:T(8,128)}, s32[]{:T(128)}, s32[]{:T(128)}) %tuple.76), condition=%wide.region_3.4_spmd.clone.clone, body=%wide.region_1.3_spmd.clone.clone.sunk | while | flops 673538 | bytes 332917 | solution.py:32
  124.3 1.0 convolution_bitcast_fusion.8
  127.1 1.0 convolution_bitcast_fusion.8
  129.9 1.0 convolution_bitcast_fusion.8
  132.8 1.0 convolution_bitcast_fusion.8
  135.6 1.0 convolution_bitcast_fusion.8
  138.5 1.0 convolution_bitcast_fusion.8
  141.3 1.0 convolution_bitcast_fusion.8
  144.1 1.0 convolution_bitcast_fusion.8
  166.8 1.0 convolution_bitcast_fusion.8
  169.7 1.0 convolution_bitcast_fusion.8
  220.8 1.0 convolution_bitcast_fusion.8
  223.6 1.0 convolution_bitcast_fusion.8
  274.7 1.0 convolution_bitcast_fusion.8
  277.5 1.0 convolution_bitcast_fusion.8
  328.6 1.0 convolution_bitcast_fusion.8
  331.5 1.0 convolution_bitcast_fusion.8
  382.6 1.0 convolution_bitcast_fusion.8
  385.4 1.0 convolution_bitcast_fusion.8
  436.5 1.0 convolution_bitcast_fusion.8
  439.3 1.0 convolution_bitcast_fusion.8
  484.8 1.3 convolution_bitcast_fusion.5
  486.9 217.1 %while.31 = (s32[]{:T(128)}, f32[128,128]{1,0:T(8,128)S(1)}, f32[128,128]{1,0:T(8,128)S(1)}, s32[]{:T(128)}, s32[]{:T(128)}, /*index=5*/s32[]{:T(128)}) while((s32[]{:T(128)}, f32[128,128]{1,0:T(8,128)S(1)}, f32[128,128]{1,0:T(8,128)S(1)}, s32[]{:T(128)}, s32[]{:T(128)}, /*index=5*/s32[]{:T(128)}) %tuple.91), condition=%wide.region_7.0_spmd.clone.clone, body=%wide.region_5.0_spmd.clone.clone.sunk | while | flops 460291 | bytes 265336 | solution.py:48
  704.1 1.5 bitcast_negate_fusion
  708.9 1.0 fusion.41
  710.5 256.7 %all-reduce.11.cloned.1.call-done = f32[128,128]{1,0:T(8,128)} async-done(((f32[128,128]{1,0:T(8,128)}), f32[128,128]{1,0:T(8,128)}) %all-reduce.11.cloned.1.call-update) | async-done | bytes 65552 | tf_op jit(solution)/shard_map/psum | solution.py:80
  967.3 1.1 fusion.57
  969.1 144.9 %all-reduce.9.cloned.1.call-done = f32[128,512]{1,0:T(8,128)} async-done(((f32[128,512]{1,0:T(8,128)}), f32[128,512]{1,0:T(8,128)}) %all-reduce.9.cloned.1.call-update) | async-done | bytes 262160 | tf_op jit(solution)/shard_map/psum | solution.py:81
  1114.0 1.4 fusion.56
  1116.0 1.4 convolution_subtract_fusion
  (1301 shorter events, 469.4 us)
Async XLA Ops:
  7.2 2.4 copy-start
  7.2 114.2 %all-reduce.7.cloned.1.call-start = ((), (), s32[]{:S(2)}) async-start(), calls=%async_computation | async-start | bytes 131072 | tf_op jit(solution)/shard_map/psum | solution.py:62
  9.5 694.5 %all-reduce.13.cloned.1.call-start = ((), (), s32[]{:S(2)}) async-start(), calls=%async_computation.3 | async-start | bytes 917504 | tf_op jit(solution)/shard_map/psum | solution.py:62
  10.2 474.6 %copy-start.1 = (f32[256,512]{1,0:T(8,128)S(1)}, f32[256,512]{1,0:T(8,128)}, u32[]{:S(2)}) copy-start(f32[256,512]{1,0:T(8,128)} %param.6) | copy-start | bytes 1572868
  486.8 480.4 %all-reduce.11.cloned.1.call-start = ((), (), s32[]{:S(2)}) async-start(), calls=%async_computation.2 | async-start | bytes 131072 | tf_op jit(solution)/shard_map/psum | solution.py:80
  707.4 1.0 copy-start.3
  708.9 1.0 copy-start.2
  709.9 404.1 %all-reduce.9.cloned.1.call-start = ((), (), s32[]{:S(2)}) async-start(), calls=%async_computation.1 | async-start | bytes 524288 | tf_op jit(solution)/shard_map/psum | solution.py:81
  710.5 257.9 %copy-start.4 = (f32[256,128]{0,1:T(8,128)S(1)}, f32[256,128]{0,1:T(8,128)}, u32[]{:S(2)}) copy-start(f32[256,128]{0,1:T(8,128)} %get-tuple-element.234) | copy-start | bytes 393220
Sparse Core Ops, SparseCore 0:
  10.9 110.4 all-reduce.6
  487.0 113.3 all-reduce.12
  710.0 257.1 all-reduce.10
  971.5 142.4 all-reduce.8
where the time goes:
time: 1140 us; the launch traced here: 1120 us
  waiting for transfers between devices  513 us (45%)
  matrix products  469 us (41%)
  loops' own time  98.4 us (9%)
  other arithmetic  28.9 us (3%)
  between operations  14 us (1%)
    dot_general x663, matrix products, multiply(): return jnp.dot(left_mat, right_mat, precision=lax.Precision.HIGHEST)  469 us
    psum x1, waiting for transfers between devices, per_device(): curv = lax.psum(multiply(left_part, refl_col), ('row', 'col'))  257 us
    psum x1, waiting for transfers between devices, per_device(): left = lax.psum(left_part, 'row')  145 us
    psum x2, waiting for transfers between devices, per_device(): gram, first = lax.psum((partial_gram, top * first_col), 'col')  111 us
    another operation x1, loops' own time, factor_lower(): return lax.fori_loop(0, width, column_step, jnp.zeros_like(gram))  94 us
  transfers between devices with their start and end apart: 4, of which 3 were waited for; matrix products, arithmetic and copies ran while one was open for 19% of the time, Pallas kernels for 0%

commit v1 on v0

v1 whole, which is shorter than its diff:
```python
import functools

import jax
import jax.numpy as jnp
from jax import lax
from jax.experimental import pallas as pl
from jax.experimental.pallas import tpu as pltpu
from jax.sharding import PartitionSpec as P

F = jnp.float32
MESH = pl.DeviceIdType.MESH
NX, NY, NC = 4, 8, 16


def dot(a, b, ca=1, cb=0):
    return lax.dot_general(
        a, b, (((ca,), (cb,)), ((), ())), precision=lax.Precision.HIGHEST, preferred_element_type=F
    )


def split(v):
    high = v.astype(jnp.bfloat16).astype(F)
    rest = v - high
    mid = rest.astype(jnp.bfloat16).astype(F)
    return high, mid, rest - mid


def dot_short(a, b):
    ah, am, al = split(a)
    bh, bm, bl = split(b)
    left = jnp.concatenate([ah, ah, am, am, ah, al], 0).astype(jnp.bfloat16)
    right = jnp.concatenate([bh, bm, bh, bm, bl, bh], 0).astype(jnp.bfloat16)
    return lax.dot_general(left, right, (((0,), (0,)), ((), ())), preferred_element_type=F)


def spread(v, i):
    return jnp.broadcast_to(v[i : i + 1, :], v.shape)


def identity(n):
    return (
        lax.broadcasted_iota(jnp.int32, (n, n), 0) == lax.broadcasted_iota(jnp.int32, (n, n), 1)
    ).astype(F)


def factor(m_ref, hooks):
    n = m_ref.shape[0]
    sub = lax.broadcasted_iota(jnp.int32, (8, n), 0)
    for b in range(n // 8):
        lo = 8 * b
        left = m_ref[lo : lo + 8, :n]
        right = m_ref[lo : lo + 8, n:]
        cols = [jnp.broadcast_to(left[:, lo + k : lo + k + 1], (8, n)) for k in range(8)]
        pivots = jnp.ones((8, n), F)
        for i in range(8):
            pivot = spread(cols[i], i)
            pivots = jnp.where(sub == i, pivot, pivots)
            if i < 7:
                mult = jnp.where(sub > i, cols[i] / pivot, 0.0)
                for k in range(i + 1, 8):
                    cols[k] = cols[k] - mult * spread(cols[k], i)
                left = left - mult * spread(left, i)
                right = right - mult * spread(right, i)
        scale = lax.rsqrt(pivots)
        left = left * scale
        both = jnp.concatenate([left, right * scale], 1)
        m_ref[lo : lo + 8, :] = both
        if lo + 8 < n:
            m_ref[lo + 8 :, :] = m_ref[lo + 8 :, :] - dot_short(left, both)[lo + 8 :]
        if b in hooks:
            hooks[b]()


def invert(m_ref, hooks):
    n = m_ref.shape[0]
    sub = lax.broadcasted_iota(jnp.int32, (8, n), 0)
    for b in range(n // 8):
        lo = 8 * b
        left = m_ref[lo : lo + 8, :n]
        right = m_ref[lo : lo + 8, n:]
        cols = [jnp.broadcast_to(left[:, lo + k : lo + k + 1], (8, n)) for k in range(8)]
        for i in range(8):
            inverse = 1.0 / spread(cols[i], i)
            mult = jnp.where(sub == i, 1.0 - inverse, cols[i] * inverse)
            for k in range(i + 1, 8):
                cols[k] = cols[k] - mult * spread(cols[k], i)
            left = left - mult * spread(left, i)
            right = right - mult * spread(right, i)
        both = jnp.concatenate([left, right], 1)
        parts = [both]
        if lo:
            parts.insert(0, jnp.zeros((lo, 2 * n), F))
        if lo + 8 < n:
            parts.append(jnp.zeros((n - lo - 8, 2 * n), F))
        m_ref[...] = m_ref[...] - dot(m_ref[:, :n], jnp.concatenate(parts, 0))
        m_ref[lo : lo + 8, :] = both
        if b in hooks:
            hooks[b]()


def kernel(
    a_ref, p_ref, out_ref, band_ref,
    prow, gsrc, grecv, pone, gall, xsrc, xrecv, aleft, xall,
    lsrc, lxrecv, lysrc, lyrecv, tsrc, tblock, tchunk, mall, zown, zy, zx, zall, work, work2,
    zsend, zrecv, xsend, xrecv_sem, ysend, yrecv_sem, psend, precv,
):
    n = p_ref.shape[1]
    rix, cix = lax.axis_index("row"), lax.axis_index("col")
    x, y = lax.div(rix, NY), lax.rem(rix, NY)
    core = lax.rem(cix, 2)

    def zpeer(k):
        return lax.rem(cix + k, NC)

    def xpeer(k):
        return lax.rem(x + k, NX) * NY + y

    def ypeer(k):
        return x * NY + lax.rem(y + k, NY)

    def zcopy(ph, k, src, dst):
        return pltpu.make_async_remote_copy(
            src_ref=src, dst_ref=dst, send_sem=zsend.at[ph, k], recv_sem=zrecv.at[ph, k],
            device_id={"col": zpeer(k)}, device_id_type=MESH)

    def xcopy(ph, k, src, dst):
        return pltpu.make_async_remote_copy(
            src_ref=src, dst_ref=dst, send_sem=xsend.at[ph, k], recv_sem=xrecv_sem.at[ph, k],
            device_id={"row": xpeer(k)}, device_id_type=MESH)

    def ycopy(ph, k, src, dst):
        return pltpu.make_async_remote_copy(
            src_ref=src, dst_ref=dst, send_sem=ysend.at[ph, k], recv_sem=yrecv_sem.at[ph, k],
            device_id={"row": ypeer(k)}, device_id_type=MESH)

    def zloop(body):
        def step(j, _):
            half = lax.div(j + 1, 2)
            body(NC // 2 + jnp.where(lax.rem(j, 2) == 1, half, -half))
            return 0
        lax.fori_loop(0, NC - 1, step, 0)

    def rows(ref, index, count):
        return ref.at[pl.ds(pl.multiple_of(index * count, count), count)]

    barrier = pltpu.get_barrier_semaphore()
    zloop(lambda k: pl.semaphore_signal(barrier, inc=1, device_id={"col": zpeer(k)}, device_id_type=MESH))
    for k in range(1, NX):
        pl.semaphore_signal(barrier, inc=1, device_id={"row": xpeer(k)}, device_id_type=MESH)
    for k in range(1, NY):
        pl.semaphore_signal(barrier, inc=1, device_id={"row": ypeer(k)}, device_id_type=MESH)
    pl.semaphore_wait(barrier, NC - 1 + NX - 1 + NY - 1)

    owner = lax.div(rix, 2)
    base = lax.rem(rix, 2) * 256
    oz = lax.div(owner, 2)
    z = lax.div(cix, 2)

    def pcopy(slot, half_src, src, peer):
        return pltpu.make_async_remote_copy(
            src_ref=src, dst_ref=rows(prow, half_src, 128), send_sem=psend.at[slot], recv_sem=precv.at[half_src],
            device_id={"col": peer}, device_id_type=MESH)

    def psource(half):
        return p_ref.at[pl.ds(pl.multiple_of(base + half * 128, 128), 128)]

    @pl.when(cix == owner)
    def _():
        def step(j, _):
            half = lax.div(j + 1, 2)
            dz = 4 + jnp.where(lax.rem(j, 2) == 1, half, -half)
            chip = lax.rem(z + dz, 8)
            for h in range(2):
                pcopy(2 * dz + h, h, psource(h), chip * 2 + h).start()
            return 0
        lax.fori_loop(0, 7, step, 0)
        for h in range(2):
            pcopy(h, h, psource(h), z * 2 + 1 - core).start()
        prow[...] = p_ref[pl.ds(pl.multiple_of(base, 256), 256), :]

    @pl.when(cix == 0)
    def _():
        zloop(lambda k: zcopy(0, k, rows(p_ref, zpeer(k), 8), pone).start())
        zloop(lambda k: zcopy(1, k, a_ref.at[pl.ds(pl.multiple_of(zpeer(k) * 16, 16), 16), pl.ds(0, 128)], aleft).start())
        pone[...] = p_ref[0:8, :]
        aleft[...] = a_ref[0:16, 0:128]

    gsrc[...] = dot(p_ref[...], p_ref[...], 0, 0)
    zloop(lambda k: zcopy(2, k, rows(gsrc, zpeer(k), 8), grecv.at[cix]).start())
    grecv[cix] = gsrc[pl.ds(pl.multiple_of(cix * 8, 8), 8), :]

    xsrc[...] = dot(a_ref[...], p_ref[...])
    zloop(lambda k: zcopy(3, k, rows(xsrc, zpeer(k), 16), xrecv.at[cix]).start())
    xrecv[cix] = xsrc[pl.ds(pl.multiple_of(cix * 16, 16), 16), :]

    @pl.when(rix == 0)
    def _():
        tsrc[...] = a_ref[0:128, :].T
        for k in range(1, NX):
            xcopy(0, k, rows(tsrc, k, 128), tblock).start()
        tblock[...] = tsrc[0:128, :]

    @pl.when(cix != 0)
    def _():
        zcopy(0, cix, pone, pone).wait_recv()
    zloop(lambda k: zcopy(2, k, grecv.at[0], grecv.at[0]).wait_recv())
    gall[cix, :, :n] = jnp.sum(grecv[...], axis=0)
    gall[cix, :, n:] = pone[...]
    zloop(lambda k: zcopy(4, k, gall.at[cix], gall.at[cix]).start())

    @pl.when(z != oz)
    def _():
        pcopy(0, core, rows(prow, core, 128), 0).wait_recv()
        pcopy(0, core, rows(prow, core, 128), z * 2 + 1 - core).start()
        pcopy(0, 1 - core, rows(prow, 1 - core, 128), 0).wait_recv()

    @pl.when((z == oz) & (cix != owner))
    def _():
        for h in range(2):
            pcopy(0, h, rows(prow, h, 128), 0).wait_recv()

    lsrc[...] = dot(a_ref[...], prow[...], 0, 0)
    for k in range(1, NX):
        xcopy(1, k, rows(lsrc, lax.rem(x + k, NX), 128), lxrecv.at[x]).start()
    lxrecv[x] = lsrc[pl.ds(pl.multiple_of(x * 128, 128), 128), :]

    @pl.when(cix != 0)
    def _():
        zcopy(1, cix, aleft, aleft).wait_recv()
    zloop(lambda k: zcopy(3, k, xrecv.at[0], xrecv.at[0]).wait_recv())
    xall[cix, :, :n] = jnp.sum(xrecv[...], axis=0)
    xall[cix, :, n:] = aleft[...]
    zloop(lambda k: zcopy(5, k, xall.at[cix], xall.at[cix]).start())

    @pl.when(y == 0)
    def _():
        @pl.when(x != 0)
        def _():
            xcopy(0, x, tblock, tblock).wait_recv()
        for k in range(1, NY):
            ycopy(0, k, rows(tblock, k, 16), tchunk).start()
        tchunk[...] = tblock[0:16, :]

    zloop(lambda k: zcopy(4, k, gall.at[0], gall.at[0]).wait_recv())
    work[:, :n] = gall[...].reshape(n, 2 * n)[:, :n]
    work[:, n:] = identity(n)

    def reduce_x():
        for k in range(1, NX):
            xcopy(1, k, lxrecv.at[0], lxrecv.at[0]).wait_recv()
        lysrc[...] = jnp.sum(lxrecv[...], axis=0)
        for k in range(1, NY):
            ycopy(1, k, rows(lysrc, lax.rem(y + k, NY), 16), lyrecv.at[y]).start()
        lyrecv[y] = lysrc[pl.ds(pl.multiple_of(y * 16, 16), 16), :]

    factor(work, {9: reduce_x})
    eye = identity(n)
    upper_mask = lax.broadcasted_iota(jnp.int32, (n, n), 0) <= lax.broadcasted_iota(jnp.int32, (n, n), 1)
    band_ref[...] = jnp.where(upper_mask, -work[:, :n], 0.0)
    first = (cix == 0).astype(F)
    top = (rix == 0).astype(F)
    t = work[:, n:]
    yrow = dot(prow[...], t, 1, 1)
    yrow = jnp.concatenate([yrow[:n] + top * eye, yrow[n:]], 0)
    work2[:, :n] = dot(gall[...].reshape(n, 2 * n)[:, n:], t, 1, 1) + eye
    work2[:, n:] = eye

    zloop(lambda k: zcopy(5, k, xall.at[0], xall.at[0]).wait_recv())
    xa = xall[...].reshape(256, 2 * n)
    nrow = dot(xa[:, :n], t, 1, 1) + xa[:, n:]
    xsrc2 = dot(yrow, nrow, 0, 0)
    zown[...] = xsrc2
    zy[y] = zown[pl.ds(pl.multiple_of(cix * 8, 8), 8), :]
    for k in range(1, NY):
        ycopy(2, k, zy.at[y], zy.at[y]).start()

    def gather_y():
        @pl.when(y != 0)
        def _():
            ycopy(0, y, tchunk, tchunk).wait_recv()
        for k in range(1, NY):
            ycopy(1, k, lyrecv.at[0], lyrecv.at[0]).wait_recv()
        mall[x, pl.ds(pl.multiple_of(y * 16, 16), 16), :] = (
            dot(jnp.sum(lyrecv[...], axis=0), work[:, n:], 1, 1) + tchunk[...]
        )
        part = mall.at[x, pl.ds(pl.multiple_of(y * 16, 16), 16)]
        for k in range(1, NY):
            ycopy(3, k, part, part).start()

    def z_x():
        for k in range(1, NY):
            ycopy(2, k, zy.at[0], zy.at[0]).wait_recv()
        zx[x] = jnp.sum(zy[...], axis=0)
        for k in range(1, NX):
            xcopy(2, k, zx.at[x], zx.at[x]).start()

    def z_col():
        for k in range(1, NX):
            xcopy(2, k, zx.at[0], zx.at[0]).wait_recv()
        zall[cix] = jnp.sum(zx[...], axis=0)
        zloop(lambda k: zcopy(6, k, zall.at[cix], zall.at[cix]).start())

    def gather_x():
        part = mall.at[0, pl.ds(0, 16)]
        for k in range(1, NY):
            ycopy(3, k, part, part).wait_recv()
        for k in range(1, NX):
            xcopy(3, k, mall.at[x], mall.at[x]).start()

    invert(work2, {2: gather_y, 7: z_x, 12: z_col, 13: gather_x})
    s = work2[:, n:]
    ycol = dot(p_ref[...], t, 1, 1)
    ycol = jnp.concatenate([ycol[:n] + first * eye, ycol[n:]], 0)
    vt = dot(ycol, s, 1, 1)
    ys = dot(yrow, s, 1, 1)
    out_ref[...] = a_ref[...] - dot(nrow, vt, 1, 1)
    zloop(lambda k: zcopy(6, k, zall.at[0], zall.at[0]).wait_recv())
    zv = dot(vt, zall[...].reshape(n, n), 1, 1)
    for k in range(1, NX):
        xcopy(3, k, mall.at[0], mall.at[0]).wait_recv()
    out_ref[...] = out_ref[...] - dot(ys, mall[...].reshape(512, n) - zv, 1, 1)

    @pl.when(cix == owner)
    def _():
        lax.fori_loop(0, 16, lambda k, _: (pcopy(k, 0, psource(0), 0).wait_send(), 0)[1], 0)

    @pl.when(z != oz)
    def _():
        pcopy(0, core, rows(prow, core, 128), 0).wait_send()

    @pl.when(cix == 0)
    def _():
        zloop(lambda k: zcopy(0, k, pone, pone).wait_send())
        zloop(lambda k: zcopy(1, k, aleft, aleft).wait_send())
    for ph, ref in ((2, grecv), (3, xrecv), (4, gall), (5, xall), (6, zall)):
        zloop(lambda k: zcopy(ph, k, ref.at[0], ref.at[0]).wait_send())

    @pl.when(rix == 0)
    def _():
        for k in range(1, NX):
            xcopy(0, k, tblock, tblock).wait_send()

    @pl.when(y == 0)
    def _():
        for k in range(1, NY):
            ycopy(0, k, tchunk, tchunk).wait_send()
    for ph, ref in ((1, lxrecv), (2, zx), (3, mall)):
        for k in range(1, NX):
            xcopy(ph, k, ref.at[0], ref.at[0]).wait_send()
    for ph, ref in ((1, lyrecv.at[0]), (2, zy.at[0]), (3, mall.at[0, pl.ds(0, 16)])):
        for k in range(1, NY):
            ycopy(ph, k, ref, ref).wait_send()


def per_device(matrix, panel):
    vm = lambda *shape: pltpu.VMEM(shape, F)
    return pl.pallas_call(
        kernel,
        out_shape=(jax.ShapeDtypeStruct((256, 512), F), jax.ShapeDtypeStruct((128, 128), F)),
        in_specs=[pl.BlockSpec(memory_space=pltpu.VMEM)] * 2,
        out_specs=(pl.BlockSpec(memory_space=pltpu.VMEM),) * 2,
        scratch_shapes=[
            vm(256, 128), vm(128, 128), vm(16, 8, 128), vm(8, 128), vm(16, 8, 256),
            vm(256, 128), vm(16, 16, 128), vm(16, 128), vm(16, 16, 256),
            vm(512, 128), vm(4, 128, 128), vm(128, 128), vm(8, 16, 128), vm(512, 128), vm(128, 128), vm(16, 128),
            vm(4, 128, 128), vm(128, 128), vm(8, 8, 128), vm(4, 8, 128), vm(16, 8, 128), vm(128, 256), vm(128, 256),
            pltpu.SemaphoreType.DMA((7, 16)), pltpu.SemaphoreType.DMA((7, 16)),
            pltpu.SemaphoreType.DMA((4, 4)), pltpu.SemaphoreType.DMA((4, 4)),
            pltpu.SemaphoreType.DMA((4, 8)), pltpu.SemaphoreType.DMA((4, 8)),
            pltpu.SemaphoreType.DMA((16,)), pltpu.SemaphoreType.DMA((2,)),
        ],
        compiler_params=pltpu.CompilerParams(collective_id=0, has_side_effects=True),
        name="panel_transform",
    )(matrix, panel)


def solution(mesh):
    placed = (P("row", "col"), P("col", None))
    return jax.shard_map(
        per_device, mesh=mesh, in_specs=placed, out_specs=(P("row", "col"), P()), check_vma=False
    )
```

time: 1140 us -> 66.2 us (0.06); the launches traced: 1120 us -> 66 us
  waiting for transfers between devices: 513 us -> 0 us
  matrix products: 469 us -> 0 us
  loops' own time: 98.4 us -> 0 us
  Pallas kernels: 0 us -> 62.8 us
  other arithmetic: 28.9 us -> 0 us
  between operations: 14 us -> 0.65 us
    psum x4 -> x0, waiting for transfers between devices: 513 us -> none  [the longest x1 257 us: per_device(): curv = lax.psum(multiply(left_part, refl_col), ('row', 'col'))]
    dot_general x663 -> x0, matrix products: 469 us -> none  [multiply(): return jnp.dot(left_mat, right_mat, precision=lax.Precision.HIGHEST)]
    another operation x2 -> x0, loops' own time: 98.4 us -> none  [the longest x1 94 us: factor_lower(): return lax.fori_loop(0, width, column_step, jnp.zeros_like(gram))]
    pallas_call x0 -> x1, Pallas kernels: none -> 62.8 us  [per_device(): pl.pallas_call(kernel, out_shape=(jax.ShapeDtypeStruct((256, 512), F), ja...]
    add x384 -> x0, other arithmetic: 25.1 us -> none  [the longest x128 13.4 us: row_step(): return inverse + unit[:, None] * solved[None, :]]
  transfers between devices with their start and end apart: 4 -> 0, of which waited for: 3 -> 0; matrix products, arithmetic and copies ran while one was open for 19% -> 0% of each run, Pallas kernels for 0% -> 0%
where the time goes in v1:
time: 66.2 us; the launch traced here: 66 us
  Pallas kernels  62.8 us (95%)
  local copies, waits for them, and re-layouts  2.53 us (4%)
    pallas_call x1, Pallas kernels, per_device(): pl.pallas_call(kernel, out_shape=(jax.ShapeDtypeStruct((256, 512), F), ja...  62.8 us
    unnamed x4, local copies, waits for them, and re-layouts  2.53 us

profile of v1, /device:TPU:1, one launch (start us, length us, event | category | flops | bytes accessed | tf_op | source)
XLA Modules:
  0.0 66.0 jit_solution(12620080119222551719)
XLA Ops:
  0.6 62.8 %panel_transform.1 = (f32[256,512]{1,0:T(8,128)}, f32[128,128]{1,0:T(8,128)}) custom-call(f32[256,512]{1,0:T(8,128)} %a_ref.1, f32[512,128]{1,0:T(8,128)} %p_ref.1), custom_call_target="tpu_custom_call" | custom-call | tf_op jit(solution)/shard_map/panel_transform/pallas_call | solution.py:357
  63.5 0.0 copy-start
  63.5 1.9 %copy.6 = f32[256,512]{1,0:T(8,128)} copy(f32[256,512]{1,0:T(8,128)} %get-tuple-element.4) | data formatting | bytes 1048576
  65.4 0.0 copy-done
  65.4 0.6 copy.7
Async XLA Ops:
  63.5 1.9 %copy-start = (f32[128,128]{1,0:T(8,128)S(1)}, f32[128,128]{1,0:T(8,128)}, u32[]{:S(2)}) copy-start(f32[128,128]{1,0:T(8,128)} %get-tuple-element.5) | copy-start | bytes 196612

commit v2 on v1

v2 whole, which is shorter than its diff:
```python
import functools

PLACE = {'p': 0, 'x': 1, 'pass': 2, 'l': 6, 'sx': 9, 'sp': 12, 'nd': 14, 'g1': (1, 7), 'g2': (2, 6), 'g3': (3, 5, 4)}
import jax
import jax.numpy as jnp
from jax import lax
from jax.experimental import pallas as pl
from jax.experimental.pallas import tpu as pltpu
from jax.sharding import PartitionSpec as P

F = jnp.float32
MESH = pl.DeviceIdType.MESH
NX, NY, NC = 4, 8, 16


def dot(a, b, ca=1, cb=0):
    return lax.dot_general(
        a, b, (((ca,), (cb,)), ((), ())), precision=lax.Precision.HIGHEST, preferred_element_type=F
    )


def split(v):
    high = v.astype(jnp.bfloat16).astype(F)
    rest = v - high
    mid = rest.astype(jnp.bfloat16).astype(F)
    return high, mid, rest - mid


def dot_short(a, b):
    ah, am, al = split(a)
    bh, bm, bl = split(b)
    left = jnp.concatenate([ah, ah, am, am, ah, al], 0).astype(jnp.bfloat16)
    right = jnp.concatenate([bh, bm, bh, bm, bl, bh], 0).astype(jnp.bfloat16)
    return lax.dot_general(left, right, (((0,), (0,)), ((), ())), preferred_element_type=F)


def spread(v, i):
    return jnp.broadcast_to(v[i : i + 1, :], v.shape)


def identity(n):
    return (
        lax.broadcasted_iota(jnp.int32, (n, n), 0) == lax.broadcasted_iota(jnp.int32, (n, n), 1)
    ).astype(F)


def factor(m_ref, hooks):
    n = m_ref.shape[0]
    sub = lax.broadcasted_iota(jnp.int32, (8, n), 0)
    for b in range(n // 8):
        lo = 8 * b
        left = m_ref[lo : lo + 8, :n]
        right = m_ref[lo : lo + 8, n:]
        cols = [jnp.broadcast_to(left[:, lo + k : lo + k + 1], (8, n)) for k in range(8)]
        pivots = jnp.ones((8, n), F)
        for i in range(8):
            pivot = spread(cols[i], i)
            pivots = jnp.where(sub == i, pivot, pivots)
            if i < 7:
                mult = jnp.where(sub > i, cols[i] / pivot, 0.0)
                for k in range(i + 1, 8):
                    cols[k] = cols[k] - mult * spread(cols[k], i)
                left = left - mult * spread(left, i)
                right = right - mult * spread(right, i)
        scale = lax.rsqrt(pivots)
        left = left * scale
        both = jnp.concatenate([left, right * scale], 1)
        m_ref[lo : lo + 8, :] = both
        if lo + 8 < n:
            m_ref[lo + 8 :, :] = m_ref[lo + 8 :, :] - dot_short(left, both)[lo + 8 :]
        if b in hooks:
            hooks[b]()


def inverse(q, doublings):
    eye = identity(q.shape[0])
    power = 0.5 * (eye - q)
    total = 0.5 * (eye + power)
    for _ in range(doublings - 1):
        power = dot(power, power)
        total = total + dot(total, power)
    return total


def kernel(
    a_hbm, p_hbm, out_ref, band_ref,
    a_ref, p_ref, prow, gsrc, grecv, pone, pall, gall, xsrc, xrecv, aleft, xall,
    lsrc, lxrecv, lysrc, lyrecv, tsrc, tblock, tchunk, mall, zown, zy, zx, zall, work, vts,
    zsend, zrecv, xsend, xrecv_sem, ysend, yrecv_sem, psend, precv, fsend, frecv, msem, asem, psem,
):
    n = p_ref.shape[1]
    rix, cix = lax.axis_index("row"), lax.axis_index("col")
    x, y = lax.div(rix, NY), lax.rem(rix, NY)
    z, core = lax.div(cix, 2), lax.rem(cix, 2)

    def zpeer(k):
        return lax.rem(cix + k, NC)

    def xpeer(k):
        return lax.rem(x + k, NX) * NY + y

    def ypeer(k):
        return x * NY + lax.rem(y + k, NY)

    def zcopy(ph, k, src, dst):
        return pltpu.make_async_remote_copy(
            src_ref=src, dst_ref=dst, send_sem=zsend.at[ph], recv_sem=zrecv.at[ph],
            device_id={"col": zpeer(k)}, device_id_type=MESH)

    def xcopy(ph, k, src, dst):
        return pltpu.make_async_remote_copy(
            src_ref=src, dst_ref=dst, send_sem=xsend.at[ph], recv_sem=xrecv_sem.at[ph],
            device_id={"row": xpeer(k)}, device_id_type=MESH)

    def ycopy(ph, k, src, dst):
        return pltpu.make_async_remote_copy(
            src_ref=src, dst_ref=dst, send_sem=ysend.at[ph], recv_sem=yrecv_sem.at[ph],
            device_id={"row": ypeer(k)}, device_id_type=MESH)

    def mcopy(k, src, dst):
        return pltpu.make_async_remote_copy(
            src_ref=src, dst_ref=dst, send_sem=ysend.at[3], recv_sem=msem.at[k],
            device_id={"row": ypeer(k)}, device_id_type=MESH)

    def fcopy(j, k, src, dst):
        return pltpu.make_async_remote_copy(
            src_ref=src, dst_ref=dst, send_sem=fsend.at[k], recv_sem=frecv.at[k],
            device_id={"row": xpeer(k)}, device_id_type=MESH)

    def zloop(body):
        for k in (8, 9, 7, 10, 6, 11, 5, 12, 4, 13, 3, 14, 2, 15, 1):
            body(k)

    def rows(ref, index, count):
        return ref.at[pl.ds(pl.multiple_of(index * count, count), count)]

    waits = {}

    def begin(name, recv, send):
        waits[name] = [recv, send]

    def recv(name):
        waits[name][0]()
        waits[name][0] = None

    def drain():
        for first_wait, last_wait in waits.values():
            if first_wait is not None:
                first_wait()
            last_wait()

    def landed(copy, ph, ref):
        return lambda: copy(ph, 1, ref, ref).wait_recv()

    def left(copy, ph, ref):
        return lambda: copy(ph, 1, ref, ref).wait_send()

    def group(name, copy, ph, ref):
        begin(name, landed(copy, ph, ref), left(copy, ph, ref))

    def only(cond, f):
        return lambda: pl.when(cond)(f)

    pin = [pltpu.make_async_copy(p_hbm.at[pl.ds(128 * k, 128)], p_ref.at[pl.ds(128 * k, 128)], psem.at[k]) for k in range(4)]
    ain = [pltpu.make_async_copy(a_hbm.at[pl.ds(64 * k, 64)], a_ref.at[pl.ds(64 * k, 64)], asem.at[k]) for k in range(4)]
    for copy in pin + ain:
        copy.start()
    barrier = pltpu.get_barrier_semaphore()
    zloop(lambda k: pl.semaphore_signal(barrier, inc=1, device_id={"col": zpeer(k)}, device_id_type=MESH))
    for k in range(1, NX):
        pl.semaphore_signal(barrier, inc=1, device_id={"row": xpeer(k)}, device_id_type=MESH)
    for k in range(1, NY):
        pl.semaphore_signal(barrier, inc=1, device_id={"row": ypeer(k)}, device_id_type=MESH)
    for copy in pin:
        copy.wait()
    gsrc[...] = dot(p_ref[...], p_ref[...], 0, 0)
    grecv[cix] = gsrc[pl.ds(pl.multiple_of(cix * 8, 8), 8), :]
    for copy in ain:
        copy.wait()
    xsrc[...] = dot(a_ref[...], p_ref[...])
    xrecv[cix] = xsrc[pl.ds(pl.multiple_of(cix * 16, 16), 16), :]
    pl.semaphore_wait(barrier, NC - 1 + NX - 1 + NY - 1)

    zloop(lambda k: zcopy(2, k, rows(gsrc, zpeer(k), 8), grecv.at[cix]).start())
    group("gram", zcopy, 2, grecv.at[pl.ds(0, 15)])

    owner = lax.div(rix, 2)
    base = lax.rem(rix, 2) * 256
    oz = lax.div(owner, 2)

    def pcopy(slot, half_src, src, peer):
        return pltpu.make_async_remote_copy(
            src_ref=src, dst_ref=src if src is a_ref else rows(prow, half_src, 128), send_sem=psend.at[slot], recv_sem=precv.at[half_src],
            device_id={"col": peer}, device_id_type=MESH)

    def psource(half):
        return p_ref.at[pl.ds(pl.multiple_of(base + half * 128, 128), 128)]

    def send_panel():
        @pl.when(cix == owner)
        def _():
            for dz in (4, 5, 3, 6, 2, 7, 1):
                chip = lax.rem(z + dz, 8)
                for h in range(2):
                    pcopy(h, h, psource(h), chip * 2 + h).start()
            for h in range(2):
                pcopy(h, h, psource(h), z * 2 + 1 - core).start()
            prow[...] = p_ref[pl.ds(pl.multiple_of(base, 256), 256), :]

    def pass_panel():
        @pl.when(z != oz)
        def _():
            pcopy(0, core, rows(prow, core, 128), 0).wait_recv()
            pcopy(2, core, rows(prow, core, 128), z * 2 + 1 - core).start()

    def prow_recv():
        @pl.when(z != oz)
        def _():
            pcopy(0, 1 - core, rows(prow, 1 - core, 128), 0).wait_recv()

        @pl.when((z == oz) & (cix != owner))
        def _():
            for h in range(2):
                pcopy(0, h, rows(prow, h, 128), 0).wait_recv()

    def prow_send():
        @pl.when(cix == owner)
        def _():
            for h in range(2):
                pcopy(h, h, a_ref, 0).wait_send()

        @pl.when(z != oz)
        def _():
            pcopy(2, core, rows(prow, core, 128), 0).wait_send()

    begin("prow", prow_recv, prow_send)

    def send_leading():
        @pl.when(cix == 0)
        def _():
            zloop(lambda k: zcopy(0, k, rows(p_ref, zpeer(k), 8), pone).start())
            zloop(lambda k: zcopy(1, k, a_ref.at[pl.ds(pl.multiple_of(zpeer(k) * 16, 16), 16), pl.ds(0, 128)], aleft).start())
            pone[...] = p_ref[0:8, :]
            aleft[...] = a_ref[0:16, 0:128]

    begin("pone", only(cix != 0, landed(zcopy, 0, pone)), only(cix == 0, left(zcopy, 0, p_ref.at[pl.ds(0, 120)])))
    begin("aleft", only(cix != 0, landed(zcopy, 1, aleft)), only(cix == 0, left(zcopy, 1, xrecv.at[pl.ds(0, 15)])))

    def send_x():
        zloop(lambda k: zcopy(3, k, rows(xsrc, zpeer(k), 16), xrecv.at[cix]).start())
        group("x", zcopy, 3, xrecv.at[pl.ds(0, 15)])

    if PLACE['p'] == 0:
        send_panel()
    if PLACE['x'] == 0:
        send_leading()
        send_x()

    recv("gram")
    gall[cix] = jnp.sum(grecv[...], axis=0)
    zloop(lambda k: zcopy(4, k, gall.at[cix], gall.at[cix]).start())
    group("gall", zcopy, 4, gall.at[pl.ds(0, 15)])
    if PLACE['p'] == 1:
        send_panel()
    if PLACE['x'] == 1:
        send_leading()
        send_x()

    @pl.when(rix == 0)
    def _():
        tsrc[...] = a_ref[0:128, :].T
        for k in range(1, NX):
            xcopy(0, k, rows(tsrc, k, 128), tblock).start()
        tblock[...] = tsrc[0:128, :]
    begin("tblock", only((y == 0) & (x != 0), landed(xcopy, 0, tblock)), only(rix == 0, left(xcopy, 0, lxrecv.at[pl.ds(0, 3)])))

    def send_l():
        recv("prow")
        for k in (2, 1, 3, 0):
            block = lax.rem(x + k, NX)
            part = dot(a_ref[:, pl.ds(pl.multiple_of(block * 128, 128), 128)], prow[...], 0, 0)
            if k:
                lsrc[block] = part
                xcopy(1, k, lsrc.at[block], lxrecv.at[x]).start()
            else:
                lxrecv[x] = part
        group("lx", xcopy, 1, lxrecv.at[pl.ds(0, 3)])

    def share_panel():
        recv("pone")
        pall[cix] = pone[...]
        zloop(lambda k: zcopy(7, k, pall.at[cix], pall.at[cix]).start())
        group("pall", zcopy, 7, pall.at[pl.ds(0, 15)])
        recv("tblock")

        @pl.when(y == 0)
        def _():
            for k in range(1, NY):
                ycopy(0, k, rows(tblock, k, 16), tchunk).start()
            tchunk[...] = tblock[0:16, :]
        begin("tchunk", only(y != 0, landed(ycopy, 0, tchunk)), only(y == 0, left(ycopy, 0, tblock.at[pl.ds(0, 112)])))

    def share_x():
        recv("aleft")
        recv("x")
        xall[cix, :, :n] = jnp.sum(xrecv[...], axis=0)
        xall[cix, :, n:] = aleft[...]
        zloop(lambda k: zcopy(5, k, xall.at[cix], xall.at[cix]).start())
        group("xall", zcopy, 5, xall.at[pl.ds(0, 15)])

    def at(name):
        for b, f in ((PLACE['pass'], pass_panel), (PLACE['l'], send_l), (PLACE['sx'], share_x), (PLACE['sp'], share_panel)):
            if b == name:
                f()

    at(-2)
    recv("gall")
    at(-1)
    work[:, :n] = gall[...].reshape(n, n)
    work[:, n:] = identity(n)
    factor(work, {b: functools.partial(at, b) for b in range(16)})
    at(16)

    recv("lx")
    lysrc[...] = jnp.sum(lxrecv[...], axis=0)
    for k in range(1, NY):
        ycopy(1, k, rows(lysrc, lax.rem(y + k, NY), 16), lyrecv.at[y]).start()
    lyrecv[y] = lysrc[pl.ds(pl.multiple_of(y * 16, 16), 16), :]
    group("ly", ycopy, 1, lyrecv.at[pl.ds(0, 7)])

    eye = identity(n)
    first = (cix == 0).astype(F)
    top = (rix == 0).astype(F)
    t = work[:, n:]
    yrow = dot(prow[...], t, 1, 1)
    yrow = jnp.concatenate([yrow[:n] + top * eye, yrow[n:]], 0)
    recv("xall")
    xa = xall[...].reshape(256, 2 * n)
    nrow = dot(xa[:, :n], t, 1, 1) + xa[:, n:]
    zown[...] = dot(yrow, nrow, 0, 0)
    zy[y] = zown[pl.ds(pl.multiple_of(cix * 8, 8), 8), :]
    for k in range(1, NY):
        ycopy(2, k, zy.at[y], zy.at[y]).start()
    group("zy", ycopy, 2, zy.at[pl.ds(0, 7)])
    recv("pall")
    s = inverse(dot(pall[...].reshape(n, n), t, 1, 1), PLACE['nd'])
    ycol = dot(p_ref[...], t, 1, 1)
    ycol = jnp.concatenate([ycol[:n] + first * eye, ycol[n:]], 0)
    upper = lax.broadcasted_iota(jnp.int32, (n, n), 0) <= lax.broadcasted_iota(jnp.int32, (n, n), 1)
    band_ref[...] = jnp.where(upper, -work[:, :n], 0.0)

    def gather_y():
        recv("tchunk")
        recv("ly")
        part = mall.at[x, pl.ds(pl.multiple_of(y * 16, 16), 16)]
        part[...] = dot(jnp.sum(lyrecv[...], axis=0), work[:, n:], 1, 1) + tchunk[...]
        for k in range(1, NY):
            mcopy(k, part, part).start()
        for k in range(1, NX):
            fcopy(0, k, part, part).start()
        for k in range(1, NY):
            begin(f"m{k}", mcopy(k, tchunk, tchunk).wait_recv, lambda: None)
        waits["m1"][1] = left(ycopy, 3, tblock.at[pl.ds(0, 112)])

    def z_x():
        recv("zy")
        zx[x] = jnp.sum(zy[...], axis=0)
        for k in range(1, NX):
            xcopy(2, k, zx.at[x], zx.at[x]).start()
        group("zx", xcopy, 2, zx.at[pl.ds(0, 3)])

    def z_col():
        recv("zx")
        zall[cix] = jnp.sum(zx[...], axis=0)
        zloop(lambda k: zcopy(6, k, zall.at[cix], zall.at[cix]).start())
        group("zall", zcopy, 6, zall.at[pl.ds(0, 15)])

    def gather_x(j):
        def go():
            part = mall.at[x, pl.ds(pl.multiple_of(lax.rem(y + NY - j, NY) * 16, 16), 16)]
            recv(f"m{j}")
            for k in range(1, NX):
                fcopy(j, k, part, part).start()
        return go

    gather_y()
    z_x()
    vt = dot(ycol, s, 1, 1)
    vts[...] = vt.reshape(4, n, n)
    ys = dot(yrow, s, 1, 1)
    for j in PLACE['g1']:
        gather_x(j)()
    z_col()
    for j in PLACE['g2']:
        gather_x(j)()
    out_ref[...] = a_ref[...] - dot(nrow, vt, 1, 1)
    for j in PLACE['g3']:
        gather_x(j)()
    recv("zall")
    zfull = zall[...].reshape(n, n)
    for k in (0, 1, 3, 2):
        block = lax.rem(x + NX - k, NX)
        if k:
            fcopy(0, k, mall.at[0], mall.at[0]).wait_recv()
        rest = mall[block] - dot(vts[block], zfull, 1, 1)
        at_block = pl.ds(pl.multiple_of(block * 128, 128), 128)
        out_ref[:, at_block] = out_ref[:, at_block] - dot(ys, rest, 1, 1)

    drain()
    for k in range(1, NX):
        fcopy(0, k, mall.at[0], mall.at[0]).wait_send()


def per_device(matrix, panel):
    keep = lambda v: pltpu.with_memory_space_constraint(v, pltpu.MemorySpace.HBM)
    vm = lambda *shape: pltpu.VMEM(shape, F)
    dma = lambda *shape: pltpu.SemaphoreType.DMA(shape)
    return pl.pallas_call(
        kernel,
        out_shape=(jax.ShapeDtypeStruct((256, 512), F), jax.ShapeDtypeStruct((128, 128), F)),
        in_specs=[pl.BlockSpec(memory_space=pltpu.MemorySpace.HBM)] * 2,
        out_specs=(pl.BlockSpec(memory_space=pltpu.VMEM),) * 2,
        scratch_shapes=[
            vm(256, 512), vm(512, 128),
            vm(256, 128), vm(128, 128), vm(16, 8, 128), vm(8, 128), vm(16, 8, 128), vm(16, 8, 128),
            vm(256, 128), vm(16, 16, 128), vm(16, 128), vm(16, 16, 256),
            vm(4, 128, 128), vm(4, 128, 128), vm(128, 128), vm(8, 16, 128), vm(512, 128), vm(128, 128), vm(16, 128),
            vm(4, 128, 128), vm(128, 128), vm(8, 8, 128), vm(4, 8, 128), vm(16, 8, 128), vm(128, 256), vm(4, 128, 128),
            dma(8), dma(8), dma(3), dma(3), dma(4), dma(4), dma(3), dma(2), dma(4), dma(4), dma(8),
            dma(4), dma(4),
        ],
        compiler_params=pltpu.CompilerParams(collective_id=0, has_side_effects=True, vmem_limit_bytes=16 << 20),
        name="panel_transform",
    )(keep(matrix), keep(panel))


def solution(mesh):
    placed = (P("row", "col"), P("col", None))
    return jax.shard_map(
        per_device, mesh=mesh, in_specs=placed, out_specs=(P("row", "col"), P()), check_vma=False
    )
```

time: 66.2 us -> 62.7 us (0.947)
  Pallas kernels: 62.8 us -> 60.5 us
  local copies, waits for them, and re-layouts: 2.53 us -> 1.42 us
    pallas_call x1, Pallas kernels: 62.8 us -> 60.5 us  [per_device(): pl.pallas_call(kernel, out_shape=(jax.ShapeDtypeStruct((256, 512), F), ja...]
    unnamed x4 -> x2, local copies, waits for them, and re-layouts: 2.53 us -> 1.42 us
where the time goes in v2:
time: 62.7 us; the launch traced here: 62.5 us
  Pallas kernels  60.5 us (96%)
  local copies, waits for them, and re-layouts  1.42 us (2%)
  between operations  0.64 us (1%)
    pallas_call x1, Pallas kernels, per_device(): pl.pallas_call(kernel, out_shape=(jax.ShapeDtypeStruct((256, 512), F), ja...  60.5 us
    unnamed x2, local copies, waits for them, and re-layouts  1.42 us

profile of v2, /device:TPU:1, one launch (start us, length us, event | category | flops | bytes accessed | tf_op | source)
XLA Modules:
  0.0 62.5 jit_solution(705577831512784955)
XLA Ops:
  0.6 60.5 %panel_transform.1 = (f32[256,512]{1,0:T(8,128)S(1)}, f32[128,128]{1,0:T(8,128)S(1)}) custom-call(f32[256,512]{1,0:T(8,128)} %a_hbm.1, f32[512,128]{1,0:T(8,128)} %p_hbm.1), custom_call_target="tpu_custom_call" | custom-call | tf_op jit(solution)/shard_map/panel_transform/pallas_call | solution.py:418
  61.1 0.8 %copy.6 = f32[256,512]{1,0:T(8,128)} copy(f32[256,512]{1,0:T(8,128)S(1)} %get-tuple-element.4) | data formatting | bytes 1048576
  61.9 0.6 %copy.7 = f32[128,128]{1,0:T(8,128)} copy(f32[128,128]{1,0:T(8,128)S(1)} %get-tuple-element.5) | data formatting | bytes 131072

commit v3 on v2

--- a/solution.py
+++ b/solution.py
@@ -1,6 +1,6 @@
 import functools
 
-PLACE = {'p': 0, 'x': 1, 'pass': 2, 'l': 6, 'sx': 9, 'sp': 12, 'nd': 14, 'g1': (1, 7), 'g2': (2, 6), 'g3': (3, 5, 4)}
+PLACE = {'p': 0, 'x': 1, 'pass': 1, 'l': 3, 'sx': 7, 'sp': 0, 'nd': 14, 'g1': (), 'g2': (1, 7), 'g3': (2, 6, 3, 5, 4)}
 import jax
 import jax.numpy as jnp
 from jax import lax
@@ -13,17 +13,23 @@
 NX, NY, NC = 4, 8, 16
 
 
-def dot(a, b, ca=1, cb=0):
-    return lax.dot_general(
-        a, b, (((ca,), (cb,)), ((), ())), precision=lax.Precision.HIGHEST, preferred_element_type=F
-    )
-
-
 def split(v):
     high = v.astype(jnp.bfloat16).astype(F)
     rest = v - high
     mid = rest.astype(jnp.bfloat16).astype(F)
     return high, mid, rest - mid
+
+
+def dot(a, b, ca=1, cb=0):
+    if ca == 0:
+        return lax.dot_general(
+            a, b, (((ca,), (cb,)), ((), ())), precision=lax.Precision.HIGHEST, preferred_element_type=F
+        )
+    ah, am, al = [v.astype(jnp.bfloat16) for v in split(a)]
+    bh, bm, bl = [v.astype(jnp.bfloat16) for v in split(b)]
+    left = jnp.concatenate([ah, ah, am, am, ah, al], ca)
+    right = jnp.concatenate([bh, bm, bh, bm, bl, bh], cb)
+    return lax.dot_general(left, right, (((ca,), (cb,)), ((), ())), preferred_element_type=F)
 
 
 def dot_short(a, b):
@@ -255,6 +261,8 @@
     if PLACE['x'] == 0:
         send_leading()
         send_x()
+    if PLACE['p'] == 2:
+        send_panel()
 
     recv("gram")
     gall[cix] = jnp.sum(grecv[...], axis=0)
@@ -334,6 +342,13 @@
     t = work[:, n:]
     yrow = dot(prow[...], t, 1, 1)
     yrow = jnp.concatenate([yrow[:n] + top * eye, yrow[n:]], 0)
+    recv("pall")
+    s = inverse(dot(pall[...].reshape(n, n), t, 1, 1), PLACE['nd'])
+    ycol = dot(p_ref[...], t, 1, 1)
+    ycol = jnp.concatenate([ycol[:n] + first * eye, ycol[n:]], 0)
+    vt = dot(ycol, s, 1, 1)
+    vts[...] = vt.reshape(4, n, n)
+    ys = dot(yrow, s, 1, 1)
     recv("xall")
     xa = xall[...].reshape(256, 2 * n)
     nrow = dot(xa[:, :n], t, 1, 1) + xa[:, n:]
@@ -342,10 +357,6 @@
     for k in range(1, NY):
         ycopy(2, k, zy.at[y], zy.at[y]).start()
     group("zy", ycopy, 2, zy.at[pl.ds(0, 7)])
-    recv("pall")
-    s = inverse(dot(pall[...].reshape(n, n), t, 1, 1), PLACE['nd'])
-    ycol = dot(p_ref[...], t, 1, 1)
-    ycol = jnp.concatenate([ycol[:n] + first * eye, ycol[n:]], 0)
     upper = lax.broadcasted_iota(jnp.int32, (n, n), 0) <= lax.broadcasted_iota(jnp.int32, (n, n), 1)
     band_ref[...] = jnp.where(upper, -work[:, :n], 0.0)
 
@@ -384,16 +395,13 @@
         return go
 
     gather_y()
-    z_x()
-    vt = dot(ycol, s, 1, 1)
-    vts[...] = vt.reshape(4, n, n)
-    ys = dot(yrow, s, 1, 1)
     for j in PLACE['g1']:
         gather_x(j)()
-    z_col()
+    z_x()
+    out_ref[...] = a_ref[...] - dot(nrow, vt, 1, 1)
     for j in PLACE['g2']:
         gather_x(j)()
-    out_ref[...] = a_ref[...] - dot(nrow, vt, 1, 1)
+    z_col()
     for j in PLACE['g3']:
         gather_x(j)()
     recv("zall")

time: 62.7 us -> 60.4 us (0.963)
  Pallas kernels: 60.5 us -> 58.2 us
    pallas_call x1, Pallas kernels: 60.5 us -> 58.2 us  [per_device(): pl.pallas_call(kernel, out_shape=(jax.ShapeDtypeStruct((256, 512), F), ja...]
where the time goes in v3:
time: 60.4 us; the launch traced here: 60.2 us
  Pallas kernels  58.2 us (96%)
  local copies, waits for them, and re-layouts  1.42 us (2%)
  between operations  0.64 us (1%)
    pallas_call x1, Pallas kernels, per_device(): pl.pallas_call(kernel, out_shape=(jax.ShapeDtypeStruct((256, 512), F), ja...  58.2 us
    unnamed x2, local copies, waits for them, and re-layouts  1.42 us

profile of v3, /device:TPU:1, one launch (start us, length us, event | category | flops | bytes accessed | tf_op | source)
XLA Modules:
  0.0 60.2 jit_solution(6234457436653154944)
XLA Ops:
  0.6 58.2 %panel_transform.1 = (f32[256,512]{1,0:T(8,128)S(1)}, f32[128,128]{1,0:T(8,128)S(1)}) custom-call(f32[256,512]{1,0:T(8,128)} %a_hbm.1, f32[512,128]{1,0:T(8,128)} %p_hbm.1), custom_call_target="tpu_custom_call" | custom-call | tf_op jit(solution)/shard_map/panel_transform/pallas_call | solution.py:426
  58.8 0.8 %copy.6 = f32[256,512]{1,0:T(8,128)} copy(f32[256,512]{1,0:T(8,128)S(1)} %get-tuple-element.4) | data formatting | bytes 1048576
  59.6 0.6 %copy.7 = f32[128,128]{1,0:T(8,128)} copy(f32[128,128]{1,0:T(8,128)S(1)} %get-tuple-element.5) | data formatting | bytes 131072

commit v4 on v3

--- a/solution.py
+++ b/solution.py
@@ -394,10 +394,8 @@
                 fcopy(j, k, part, part).start()
         return go
 
+    z_x()
     gather_y()
-    for j in PLACE['g1']:
-        gather_x(j)()
-    z_x()
     out_ref[...] = a_ref[...] - dot(nrow, vt, 1, 1)
     for j in PLACE['g2']:
         gather_x(j)()

time: 60.4 us -> 60 us (level)
  no operation moved by 1% of the time
where the time goes in v4:
time: 60 us; the launch traced here: 59.8 us
  Pallas kernels  57.8 us (96%)
  local copies, waits for them, and re-layouts  1.42 us (2%)
  between operations  0.64 us (1%)
    pallas_call x1, Pallas kernels, per_device(): pl.pallas_call(kernel, out_shape=(jax.ShapeDtypeStruct((256, 512), F), ja...  57.8 us
    unnamed x2, local copies, waits for them, and re-layouts  1.42 us

profile of v4, /device:TPU:1, one launch (start us, length us, event | category | flops | bytes accessed | tf_op | source)
XLA Modules:
  0.0 59.8 jit_solution(10221004433483048308)
XLA Ops:
  0.6 57.8 %panel_transform.1 = (f32[256,512]{1,0:T(8,128)S(1)}, f32[128,128]{1,0:T(8,128)S(1)}) custom-call(f32[256,512]{1,0:T(8,128)} %a_hbm.1, f32[512,128]{1,0:T(8,128)} %p_hbm.1), custom_call_target="tpu_custom_call" | custom-call | tf_op jit(solution)/shard_map/panel_transform/pallas_call | solution.py:424
  58.4 0.8 %copy.6 = f32[256,512]{1,0:T(8,128)} copy(f32[256,512]{1,0:T(8,128)S(1)} %get-tuple-element.4) | data formatting | bytes 1048576
  59.2 0.6 %copy.7 = f32[128,128]{1,0:T(8,128)} copy(f32[128,128]{1,0:T(8,128)S(1)} %get-tuple-element.5) | data formatting | bytes 131072

commit v5 on v4

--- a/solution.py
+++ b/solution.py
@@ -346,9 +346,6 @@
     s = inverse(dot(pall[...].reshape(n, n), t, 1, 1), PLACE['nd'])
     ycol = dot(p_ref[...], t, 1, 1)
     ycol = jnp.concatenate([ycol[:n] + first * eye, ycol[n:]], 0)
-    vt = dot(ycol, s, 1, 1)
-    vts[...] = vt.reshape(4, n, n)
-    ys = dot(yrow, s, 1, 1)
     recv("xall")
     xa = xall[...].reshape(256, 2 * n)
     nrow = dot(xa[:, :n], t, 1, 1) + xa[:, n:]
@@ -357,6 +354,9 @@
     for k in range(1, NY):
         ycopy(2, k, zy.at[y], zy.at[y]).start()
     group("zy", ycopy, 2, zy.at[pl.ds(0, 7)])
+    vt = dot(ycol, s, 1, 1)
+    vts[...] = vt.reshape(4, n, n)
+    ys = dot(yrow, s, 1, 1)
     upper = lax.broadcasted_iota(jnp.int32, (n, n), 0) <= lax.broadcasted_iota(jnp.int32, (n, n), 1)
     band_ref[...] = jnp.where(upper, -work[:, :n], 0.0)
 

time: 60 us -> 59.5 us (level)
  no operation moved by 1% of the time
where the time goes in v5:
time: 59.5 us; the launch traced here: 59.4 us
  Pallas kernels  57.3 us (96%)
  local copies, waits for them, and re-layouts  1.42 us (2%)
  between operations  0.64 us (1%)
    pallas_call x1, Pallas kernels, per_device(): pl.pallas_call(kernel, out_shape=(jax.ShapeDtypeStruct((256, 512), F), ja...  57.3 us
    unnamed x2, local copies, waits for them, and re-layouts  1.42 us

profile of v5, /device:TPU:1, one launch (start us, length us, event | category | flops | bytes accessed | tf_op | source)
XLA Modules:
  0.0 59.4 jit_solution(9192377890410529512)
XLA Ops:
  0.6 57.3 %panel_transform.1 = (f32[256,512]{1,0:T(8,128)S(1)}, f32[128,128]{1,0:T(8,128)S(1)}) custom-call(f32[256,512]{1,0:T(8,128)} %a_hbm.1, f32[512,128]{1,0:T(8,128)} %p_hbm.1), custom_call_target="tpu_custom_call" | custom-call | tf_op jit(solution)/shard_map/panel_transform/pallas_call | solution.py:424
  58.0 0.8 %copy.6 = f32[256,512]{1,0:T(8,128)} copy(f32[256,512]{1,0:T(8,128)S(1)} %get-tuple-element.4) | data formatting | bytes 1048576
  58.8 0.6 %copy.7 = f32[128,128]{1,0:T(8,128)} copy(f32[128,128]{1,0:T(8,128)S(1)} %get-tuple-element.5) | data formatting | bytes 131072
